TPU v7x, 256 devices: a whole 4x4x8 slice. The times are simulated.
256 devices in a mesh: lev: 8 (over z_lo, x), hor: 32 (over z_hi, y, core).
Axes of the slice: x: 4, y: 4, z: 8 (z_hi: 4, z_lo: 2; z = z_hi * 2 + z_lo), core: 2. Of those that a mesh axis runs over, the one named last changes fastest.
Arguments:
- slab_fields: float32 [4, 32, 524288], P(None, 'lev', 'hor'), may hold values from -6 to 6
- sample_index: int32 [32, 1024], P('hor', 'lev'), may hold values from 0 to 2047
- thickness: float32 [32], replicated, may hold values from 0.3 to 3
- level_cuts: int32 [31], replicated, may hold values 0 or 1
Outputs:
- gram: float32 [2176, 2176], P('hor', 'lev')
Inputs may be any that keep to these rules, and one draw needn't show every extreme that they name: sample_index[j, k] indexes a column among the 2048 columns that start at j * 16384 + (k // 128) * 2048.
All inputs are finite; a program needn't handle non-finite values.
Results may differ from a plain program's by a relative error of at most 0.00068.
Values may be sent and summed in bfloat16 or wider, within the bound.
No kernel may reach another device: no remote copies, remote signals or barrier semaphores. Data moves between devices by JAX's collectives and lax.ppermute only.
A program may use at most 128 MiB of HBM per device.

v0:
```python
import jax
import jax.numpy as jnp
from jax import lax
from jax.sharding import PartitionSpec as P


def vertical_filter(values, thickness, level_cuts):
    link = 1.0 - level_cuts.astype(jnp.float32)
    zero_one = jnp.zeros((1,), jnp.float32)
    lower_link = jnp.concatenate([zero_one, link])
    upper_link = jnp.concatenate([link, zero_one])
    lower_weight = jnp.concatenate([zero_one, thickness[:-1]]) * lower_link
    upper_weight = jnp.concatenate([thickness[1:], zero_one]) * upper_link
    zero_row = jnp.zeros_like(values[:, :1, :])
    below = jnp.concatenate([zero_row, values[:, :-1, :]], axis=1)
    above = jnp.concatenate([values[:, 1:, :], zero_row], axis=1)
    numer = (
        2.0 * thickness[None, :, None] * values
        + lower_weight[None, :, None] * below
        + upper_weight[None, :, None] * above
    )
    denom = 2.0 * thickness + lower_weight + upper_weight
    return numer / denom[None, :, None]


def quadratic_features(smooth):
    count = smooth.shape[2]
    later = jnp.concatenate([smooth[2], smooth[3]], axis=0)
    earlier = jnp.concatenate([smooth[0], smooth[1]], axis=0)
    product = (later[:, None, :] * smooth[0][None, :, :]).reshape(-1, count)
    return jnp.concatenate([later, earlier, product], axis=0).astype(jnp.bfloat16)


def on_device(slab_fields, sample_index, thickness, level_cuts):
    samp_count = sample_index.shape[1]
    lev_count = lax.axis_size("lev")
    hor_count = lax.axis_size("hor")
    all_lists = lax.all_gather(sample_index, "lev", axis=1, tiled=True)[0]
    group_cols = slab_fields.shape[2] // lev_count
    offsets = jnp.arange(all_lists.shape[0]) // samp_count * group_cols + all_lists
    chosen = jnp.take(slab_fields, offsets, axis=2)
    picked_cols = lax.all_to_all(chosen, "lev", split_axis=2, concat_axis=1, tiled=True)
    smooth = vertical_filter(picked_cols, thickness, level_cuts)
    feat_count = 4 * smooth.shape[1] + 2 * smooth.shape[1] * smooth.shape[1]
    col_count = feat_count // lev_count
    col_start = lax.axis_index("lev") * col_count
    features_bf = quadratic_features(smooth)
    block_features_bf = lax.all_gather(features_bf, "lev", axis=1, tiled=True)
    chosen_rows = lax.dynamic_slice_in_dim(block_features_bf, col_start, col_count, 0)
    column_block = lax.dot_general(
        block_features_bf, chosen_rows, (((1,), (1,)), ((), ())), preferred_element_type=jnp.float32
    )
    gram_block = lax.psum_scatter(column_block, "hor", scatter_dimension=0, tiled=True)
    count_all = samp_count * lev_count * hor_count
    return gram_block / count_all


def solution(mesh):
    in_specs = (P(None, "lev", "hor"), P("hor", "lev"), P(), P())
    out_specs = P("hor", "lev")
    return jax.shard_map(
        on_device, mesh=mesh, in_specs=in_specs, out_specs=out_specs, check_vma=False
    )
```

profile of v0, /device:TPU:26, one launch (start us, length us, event | category | flops | bytes accessed | tf_op | source)
XLA Modules:
  0.0 281.2 jit_solution(17869697223792710759)
XLA Ops:
  6.5 21.7 %copy.7 = f32[4,4,16384]{1,0,2:T(4,128)} copy(f32[4,4,16384]{2,1,0:T(4,128)} %param.4) | data formatting | bytes 2097152 | tf_op args[0]
  28.3 16.4 %all_gather.6 = s32[1,1024]{1,0:T(1,128)S(1)} all-gather(s32[1,128]{1,0:T(1,128)S(1)} %copy-done.2), channel_id=1, replica_groups=mesh['lev'=8,'hor'=32] {'lev'}, dimensions={1}, use_global_device_ids=true | all-gather | bytes 4608 | tf_op jit(solution)/shard_map/all_gather | solution.py:38
  44.7 16.8 %gather_fusion = f32[1024,4,4]{2,1,0:T(4,128)} fusion(f32[4,4,16384]{1,0,2:T(4,128)} %copy.7, s32[1024]{0:T(1024)S(1)} %broadcast_clamp_fusion), kind=kCustom, calls=%fused_computation | custom fusion | bytes 135168 | tf_op jit(solution)/shard_map/jit(_take)/gather | solution.py:41
  61.5 5.5 %fusion.18 = f32[1024,4,4]{2,1,0:T(4,128)S(1)} fusion(f32[1024,4,4]{2,1,0:T(4,128)} %gather_fusion, pred[1024]{0:T(1024)(128)(4,1)S(1)} %compare_and_fusion), kind=kLoop, calls=%fused_computation.49 | loop fusion | flops 16384 | bytes 132096
  67.0 3.0 %reshape.135 = f32[8,1,2048]{2,1,0:T(1,128)} reshape(f32[1024,4,4]{2,1,0:T(4,128)S(1)} %fusion.18) | data formatting | bytes 131072
  70.1 6.6 %all-to-all-start = ((f32[8,1,2048]{2,1,0:T(1,128)}), f32[8,1,2048]{2,1,0:T(1,128)S(1)}, u32[]{:S(2)}, u32[]{:S(2)}) async-start(f32[8,1,2048]{2,1,0:T(1,128)} %reshape.135), calls=%async_computation | async-start | bytes 131072 | tf_op jit(solution)/shard_map/all_to_all | solution.py:42
  76.7 0.1 fusion.17
  76.7 0.1 add_add_fusion
  76.8 4.8 %all-to-all-done = f32[8,1,2048]{2,1,0:T(1,128)S(1)} async-done(((f32[8,1,2048]{2,1,0:T(1,128)}), f32[8,1,2048]{2,1,0:T(1,128)S(1)}, u32[]{:S(2)}, u32[]{:S(2)}) %all-to-all-start) | async-done | bytes 65568 | tf_op jit(solution)/shard_map/all_to_all | solution.py:42
  81.6 0.5 broadcast.122
  82.1 0.8 reduce
  82.9 2.7 reshape.136
  85.6 0.8 copy.8
  86.5 0.1 add_divide_fusion
  86.6 0.1 multiply_convert_fusion
  86.7 0.1 constant_dynamic-update-slice_fusion
  86.8 0.8 copy-done
  87.6 0.0 all-gather.2.cloned.1.call-update
  87.7 64.6 %all-gather.2.cloned.1.call-done = bf16[2176,1024]{1,0:T(8,128)(2,1)} async-done(((bf16[2176,128]{1,0:T(8,128)(2,1)}), bf16[2176,1024]{1,0:T(8,128)(2,1)}) %all-gather.2.cloned.1.call-update) | async-done | bytes 4456464 | tf_op jit(solution)/shard_map/all_gather | solution.py:48
  152.2 4.9 %fusion.1 = f32[2176,272]{1,0:T(8,128)S(1)} fusion(bf16[2176,1024]{1,0:T(8,128)(2,1)} %all-gather.2.cloned.1.call-done, s32[]{:T(128)S(6)} %select_n.43), kind=kOutput, calls=%fused_computation.3 | convolution fusion | flops 1212153856 | bytes 7380996 | tf_op jit(solution)/shard_map/dot_general | solution.py:50
  157.1 0.0 copy-start.4
  157.2 75.4 %fusion = f32[80,272]{1,0:T(8,128)S(1)} fusion(f32[2176,272]{1,0:T(8,128)S(1)} %fusion.1), kind=kCustom, calls=%all-reduce-scatter | all-reduce-scatter fusion | flops 696321 | bytes 2455552
  232.6 4.4 %collective-permute-start.3 = (f32[80,272]{1,0:T(8,128)S(1)}, f32[80,272]{1,0:T(8,128)S(1)}, u32[]{:S(2)}, u32[]{:S(2)}) collective-permute-start(f32[80,272]{1,0:T(8,128)S(1)} %fusion), channel_id=1, source_target_pairs={{0,4},{1,5},{2,6},{3,7},{4,8},{5,9},{6,10},{7,11},{8,12},{9,13},{1... | collective-permute-start | bytes 261128
  236.9 8.4 %collective-permute-start.2 = (f32[80,272]{1,0:T(8,128)S(1)}, f32[80,272]{1,0:T(8,128)S(1)}, u32[]{:S(2)}, u32[]{:S(2)}) collective-permute-start(f32[80,272]{1,0:T(8,128)S(1)} %fusion), channel_id=1, source_target_pairs={{0,3},{1,4},{2,5},{3,6},{4,7},{5,8},{6,9},{7,10},{8,11},{9,12},{10... | collective-permute-start | bytes 261128
  245.3 10.9 %collective-permute-start.1 = (f32[80,272]{1,0:T(8,128)S(1)}, f32[80,272]{1,0:T(8,128)S(1)}, u32[]{:S(2)}, u32[]{:S(2)}) collective-permute-start(f32[80,272]{1,0:T(8,128)S(1)} %fusion), channel_id=1, source_target_pairs={{0,2},{1,3},{2,4},{3,5},{4,6},{5,7},{6,8},{7,9},{8,10},{9,11},{10,... | collective-permute-start | bytes 261128
  256.3 8.4 %collective-permute-start = (f32[80,272]{1,0:T(8,128)S(1)}, f32[80,272]{1,0:T(8,128)S(1)}, u32[]{:S(2)}, u32[]{:S(2)}) collective-permute-start(f32[80,272]{1,0:T(8,128)S(1)} %fusion), channel_id=1, source_target_pairs={{0,1},{1,2},{2,3},{3,4},{4,5},{5,6},{6,7},{7,8},{8,9},{9,10},{10,1... | collective-permute-start | bytes 261128
  264.7 1.9 collective-permute-start.4
  266.6 0.6 dynamic-slice.4
  267.9 4.8 %collective-permute-done.4 = f32[52,272]{1,0:T(8,128)S(1)} collective-permute-done((f32[52,272]{1,0:T(8,128)S(1)}, f32[52,272]{1,0:T(8,128)S(1)}, u32[]{:S(2)}, u32[]{:S(2)}) %collective-permute-start.4) | collective-permute-done | bytes 56608
  272.6 0.0 collective-permute-done.3
  272.7 1.0 concatenate.50
  273.7 0.7 dynamic-slice_multiply_fusion
  (23 shorter events, 0.1 us)
Async XLA Ops:
  6.5 21.7 %copy-start.2 = (s32[1,128]{1,0:T(1,128)S(1)}, s32[1,128]{1,0:T(1,128)}, u32[]{:S(2)}) copy-start(s32[1,128]{1,0:T(1,128)} %param.5) | copy-start | bytes 1540
  28.2 48.4 %copy-start.1 = (f32[32]{0:T(128)S(1)}, f32[32]{0:T(128)}, u32[]{:S(2)}) copy-start(f32[32]{0:T(128)} %param.6) | copy-start | bytes 388
  28.2 48.4 %copy-start.3 = (s32[31]{0:T(128)S(1)}, s32[31]{0:T(128)}, u32[]{:S(2)}) copy-start(s32[31]{0:T(128)} %param.7) | copy-start | bytes 376
  70.1 11.5 %all-to-all-start = ((f32[8,1,2048]{2,1,0:T(1,128)}), f32[8,1,2048]{2,1,0:T(1,128)S(1)}, u32[]{:S(2)}, u32[]{:S(2)}) async-start(f32[8,1,2048]{2,1,0:T(1,128)} %reshape.135), calls=%async_computation | async-start | bytes 131072 | tf_op jit(solution)/shard_map/all_to_all | solution.py:42
  76.6 75.6 %all-gather.2.cloned.1.call-start = ((), (), s32[]{:S(2)}) async-start(), calls=%async_computation.1 | async-start | bytes 5013504 | tf_op jit(solution)/shard_map/all_gather | solution.py:48
  86.8 0.8 copy-start
  157.1 109.5 %copy-start.4 = (u32[256]{0:T(256)S(1)}, u32[256]{0:T(256)}, u32[]{:S(2)}) copy-start(u32[256]{0:T(256)} %constant.76) | copy-start | bytes 3076
  232.6 40.1 %collective-permute-start.3 = (f32[80,272]{1,0:T(8,128)S(1)}, f32[80,272]{1,0:T(8,128)S(1)}, u32[]{:S(2)}, u32[]{:S(2)}) collective-permute-start(f32[80,272]{1,0:T(8,128)S(1)} %fusion), channel_id=1, source_target_pairs={{0,4},{1,5},{2,6},{3,7},{4,8},{5,9},{6,10},{7,11},{8,12},{9,13},{1... | collective-permute-start | bytes 261128
  236.9 35.7 %collective-permute-start.2 = (f32[80,272]{1,0:T(8,128)S(1)}, f32[80,272]{1,0:T(8,128)S(1)}, u32[]{:S(2)}, u32[]{:S(2)}) collective-permute-start(f32[80,272]{1,0:T(8,128)S(1)} %fusion), channel_id=1, source_target_pairs={{0,3},{1,4},{2,5},{3,6},{4,7},{5,8},{6,9},{7,10},{8,11},{9,12},{10... | collective-permute-start | bytes 261128
  245.3 27.3 %collective-permute-start.1 = (f32[80,272]{1,0:T(8,128)S(1)}, f32[80,272]{1,0:T(8,128)S(1)}, u32[]{:S(2)}, u32[]{:S(2)}) collective-permute-start(f32[80,272]{1,0:T(8,128)S(1)} %fusion), channel_id=1, source_target_pairs={{0,2},{1,3},{2,4},{3,5},{4,6},{5,7},{6,8},{7,9},{8,10},{9,11},{10,... | collective-permute-start | bytes 261128
  256.3 16.4 %collective-permute-start = (f32[80,272]{1,0:T(8,128)S(1)}, f32[80,272]{1,0:T(8,128)S(1)}, u32[]{:S(2)}, u32[]{:S(2)}) collective-permute-start(f32[80,272]{1,0:T(8,128)S(1)} %fusion), channel_id=1, source_target_pairs={{0,1},{1,2},{2,3},{3,4},{4,5},{5,6},{6,7},{7,8},{8,9},{9,10},{10,1... | collective-permute-start | bytes 261128
  264.7 7.9 %collective-permute-start.4 = (f32[52,272]{1,0:T(8,128)S(1)}, f32[52,272]{1,0:T(8,128)S(1)}, u32[]{:S(2)}, u32[]{:S(2)}) collective-permute-start(f32[52,272]{1,0:T(8,128)S(1)} %slice.42), channel_id=1, source_target_pairs={{0,5},{1,6},{2,7},{3,8},{4,9},{5,10},{6,11},{7,12},{8,13},{9,14},{... | collective-permute-start | bytes 169736
Sparse Core Ops, SparseCore 0:
  87.8 64.4 all-gather.1
where the time goes:
time: 284 us; the launch traced here: 281 us
  blocking collectives  91.9 us (32%)
  waiting for transfers between devices  74.1 us (26%)
  local copies, waits for them, and re-layouts  48.2 us (17%)
  starting transfers between devices  40.6 us (14%)
  between operations  14.3 us (5%)
  other arithmetic  7.31 us (3%)
  matrix products  4.9 us (2%)
    unnamed x1, blocking collectives  75.4 us
    all_gather x1, waiting for transfers between devices, on_device(): block_features_bf = lax.all_gather(features_bf, 'lev', axis=1, tiled=True)  64.6 us
    unnamed x5, starting transfers between devices  34 us
    unnamed x20, local copies, waits for them, and re-layouts  30 us
    gather x1, local copies, waits for them, and re-layouts, on_device(): chosen = jnp.take(slab_fields, offsets, axis=2)  16.8 us
    all_gather x1, blocking collectives, on_device(): all_lists = lax.all_gather(sample_index, 'lev', axis=1, tiled=True)[0]  16.4 us
    all_to_all x1, starting transfers between devices, on_device(): lax.all_to_all(chosen, 'lev', split_axis=2, concat_axis=1, tiled=True)  6.56 us
  transfers between devices with their start and end apart: 7, of which 3 were waited for; matrix products, arithmetic and copies ran while one was open for 0% of the time, Pallas kernels for 0%

commit v1 on v0

--- a/solution.py
+++ b/solution.py
@@ -39,7 +39,9 @@
     group_cols = slab_fields.shape[2] // lev_count
     offsets = jnp.arange(all_lists.shape[0]) // samp_count * group_cols + all_lists
     chosen = jnp.take(slab_fields, offsets, axis=2)
-    picked_cols = lax.all_to_all(chosen, "lev", split_axis=2, concat_axis=1, tiled=True)
+    cells = jnp.split(chosen, lax.axis_size("lev"), axis=2)
+    arrived = lax.all_to_all(jnp.stack(cells), "lev", 0, 0)
+    picked_cols = jnp.concatenate(arrived, axis=1)
     smooth = vertical_filter(picked_cols, thickness, level_cuts)
     feat_count = 4 * smooth.shape[1] + 2 * smooth.shape[1] * smooth.shape[1]
     col_count = feat_count // lev_count

time: 284 us -> 274 us (0.965)
  the two profiles are of different devices: /device:TPU:26 before, /device:TPU:171 now
where the time goes in v1:
time: 274 us; the launch traced here: 271 us
  waiting for transfers between devices  90.9 us (33%)
  blocking collectives  90.8 us (33%)
  local copies, waits for them, and re-layouts  37.7 us (14%)
  starting transfers between devices  27.9 us (10%)
  between operations  14.3 us (5%)
  matrix products  4.9 us (2%)
  other arithmetic  4.77 us (2%)
    unnamed x1, blocking collectives  78.9 us
    all_gather x1, waiting for transfers between devices, on_device(): block_features_bf = lax.all_gather(features_bf, 'lev', axis=1, tiled=True)  66.4 us
    unnamed x23, local copies, waits for them, and re-layouts  24.4 us
    unnamed x6, waiting for transfers between devices  21.4 us
    unnamed x5, starting transfers between devices  21.2 us
    all_gather x1, blocking collectives, on_device(): all_lists = lax.all_gather(sample_index, 'lev', axis=1, tiled=True)[0]  11.9 us
    gather x1, local copies, waits for them, and re-layouts, on_device(): chosen = jnp.take(slab_fields, offsets, axis=2)  11.7 us
    all_to_all x1, starting transfers between devices, on_device(): arrived = lax.all_to_all(jnp.stack(cells), 'lev', 0, 0)  6.69 us
  transfers between devices with their start and end apart: 7, of which 3 were waited for; matrix products, arithmetic and copies ran while one was open for 0% of the time, Pallas kernels for 0%

profile of v1, /device:TPU:171, one launch (start us, length us, event | category | flops | bytes accessed | tf_op | source)
XLA Modules:
  0.0 271.3 jit_solution(6795734570368282034)
XLA Ops:
  6.5 11.9 %all_gather.6 = s32[1,1024]{1,0:T(1,128)S(1)} all-gather(s32[1,128]{1,0:T(1,128)} %param.5), channel_id=1, replica_groups=mesh['lev'=8,'hor'=32] {'lev'}, dimensions={1}, use_global_device_ids=true | all-gather | bytes 4608 | tf_op jit(solution)/shard_map/all_gather | solution.py:38
  18.4 21.7 %copy.18 = f32[4,4,16384]{1,0,2:T(4,128)} copy(f32[4,4,16384]{2,1,0:T(4,128)} %param.4) | data formatting | bytes 2097152 | tf_op args[0]
  40.1 11.7 %gather_fusion = f32[1024,4,4]{2,1,0:T(4,128)S(1)} fusion(f32[4,4,16384]{1,0,2:T(4,128)} %copy.18, s32[1024]{0:T(1024)S(1)} %broadcast_clamp_fusion), kind=kCustom, calls=%fused_computation | custom fusion | bytes 135168 | tf_op jit(solution)/shard_map/jit(_take)/gather | solution.py:41
  51.9 3.7 %select_bitcast_fusion = f32[4,4,1024]{1,0,2:T(4,128)S(1)} fusion(f32[1024,4,4]{2,1,0:T(4,128)S(1)} %gather_fusion, pred[1024]{0:T(1024)(128)(4,1)S(1)} %compare_and_fusion), kind=kLoop, calls=%fused_computation.1 | loop fusion | flops 16384 | bytes 132096 | tf_op jit(solution)/shard_map/jit(_take)/select_n | solution.py:41
  55.8 0.0 copy-start.1
  55.8 0.0 copy-start.2
  56.0 1.4 copy.19
  57.4 6.7 %all-to-all-start = ((f32[8,4,4,128]{3,2,1,0:T(4,128)}), f32[8,4,4,128]{3,2,1,0:T(4,128)S(1)}, u32[]{:S(2)}, u32[]{:S(2)}) async-start(f32[8,4,4,128]{3,2,1,0:T(4,128)} %copy.19), calls=%async_computation | async-start | bytes 131072 | tf_op jit(solution)/shard_map/all_to_all | solution.py:43
  64.1 0.1 fusion.25
  64.2 0.1 add_add_fusion
  64.3 3.1 %all-to-all-done = f32[8,4,4,128]{3,2,1,0:T(4,128)S(1)} async-done(((f32[8,4,4,128]{3,2,1,0:T(4,128)}), f32[8,4,4,128]{3,2,1,0:T(4,128)S(1)}, u32[]{:S(2)}, u32[]{:S(2)}) %all-to-all-start) | async-done | bytes 65568 | tf_op jit(solution)/shard_map/all_to_all | solution.py:43
  67.4 0.1 add_divide_fusion
  67.6 0.1 multiply_convert_fusion
  67.7 0.1 constant_dynamic-update-slice_fusion
  67.8 0.8 copy-done
  68.6 0.0 all-gather.2.cloned.1.call-update
  68.6 66.4 %all-gather.2.cloned.1.call-done = bf16[2176,1024]{1,0:T(8,128)(2,1)} async-done(((bf16[2176,128]{1,0:T(8,128)(2,1)}), bf16[2176,1024]{1,0:T(8,128)(2,1)}) %all-gather.2.cloned.1.call-update) | async-done | bytes 4456464 | tf_op jit(solution)/shard_map/all_gather | solution.py:50
  135.0 4.9 %fusion.1 = f32[2176,272]{1,0:T(8,128)S(1)} fusion(bf16[2176,1024]{1,0:T(8,128)(2,1)} %all-gather.2.cloned.1.call-done, s32[]{:T(128)S(6)} %select_n.43), kind=kOutput, calls=%fused_computation.3 | convolution fusion | flops 1212153856 | bytes 7380996 | tf_op jit(solution)/shard_map/dot_general | solution.py:52
  139.9 0.0 copy-start.3
  140.0 78.9 %fusion = f32[80,272]{1,0:T(8,128)S(1)} fusion(f32[2176,272]{1,0:T(8,128)S(1)} %fusion.1), kind=kCustom, calls=%all-reduce-scatter | all-reduce-scatter fusion | flops 696321 | bytes 2455552
  218.9 3.7 %collective-permute-start = (f32[80,272]{1,0:T(8,128)S(1)}, f32[80,272]{1,0:T(8,128)S(1)}, u32[]{:S(2)}, u32[]{:S(2)}) collective-permute-start(f32[80,272]{1,0:T(8,128)S(1)} %fusion), channel_id=1, source_target_pairs={{0,1},{1,2},{2,3},{3,4},{4,5},{5,6},{6,7},{7,8},{8,9},{9,10},{10,1... | collective-permute-start | bytes 261128
  222.6 2.0 collective-permute-start.1
  224.5 9.5 %collective-permute-start.2 = (f32[80,272]{1,0:T(8,128)S(1)}, f32[80,272]{1,0:T(8,128)S(1)}, u32[]{:S(2)}, u32[]{:S(2)}) collective-permute-start(f32[80,272]{1,0:T(8,128)S(1)} %fusion), channel_id=1, source_target_pairs={{0,3},{1,4},{2,5},{3,6},{4,7},{5,8},{6,9},{7,10},{8,11},{9,12},{10... | collective-permute-start | bytes 261128
  234.0 1.9 collective-permute-start.3
  236.0 4.2 %collective-permute-start.4 = (f32[52,272]{1,0:T(8,128)S(1)}, f32[52,272]{1,0:T(8,128)S(1)}, u32[]{:S(2)}, u32[]{:S(2)}) collective-permute-start(f32[52,272]{1,0:T(8,128)S(1)} %slice.42), channel_id=1, source_target_pairs={{0,5},{1,6},{2,7},{3,8},{4,9},{5,10},{6,11},{7,12},{8,13},{9,14},{... | collective-permute-start | bytes 169736
  240.1 0.6 dynamic-slice.4
  241.4 21.4 %collective-permute-done.4 = f32[52,272]{1,0:T(8,128)S(1)} collective-permute-done((f32[52,272]{1,0:T(8,128)S(1)}, f32[52,272]{1,0:T(8,128)S(1)}, u32[]{:S(2)}, u32[]{:S(2)}) %collective-permute-start.4) | collective-permute-done | bytes 56608
  262.8 0.0 collective-permute-done
  262.8 0.0 collective-permute-done.1
  262.8 0.0 collective-permute-done.3
  262.8 1.0 concatenate.50
  263.8 0.7 dynamic-slice_multiply_fusion
  (26 shorter events, 0.4 us)
Async XLA Ops:
  55.8 8.3 %copy-start.1 = (f32[32]{0:T(128)S(1)}, f32[32]{0:T(128)}, u32[]{:S(2)}) copy-start(f32[32]{0:T(128)} %param.6) | copy-start | bytes 388
  55.8 8.3 %copy-start.2 = (s32[31]{0:T(128)S(1)}, s32[31]{0:T(128)}, u32[]{:S(2)}) copy-start(s32[31]{0:T(128)} %param.7) | copy-start | bytes 376
  57.4 10.0 %all-to-all-start = ((f32[8,4,4,128]{3,2,1,0:T(4,128)}), f32[8,4,4,128]{3,2,1,0:T(4,128)S(1)}, u32[]{:S(2)}, u32[]{:S(2)}) async-start(f32[8,4,4,128]{3,2,1,0:T(4,128)} %copy.19), calls=%async_computation | async-start | bytes 131072 | tf_op jit(solution)/shard_map/all_to_all | solution.py:43
  64.1 70.9 %all-gather.2.cloned.1.call-start = ((), (), s32[]{:S(2)}) async-start(), calls=%async_computation.1 | async-start | bytes 5013504 | tf_op jit(solution)/shard_map/all_gather | solution.py:50
  67.8 0.8 copy-start
  139.9 100.2 %copy-start.3 = (u32[256]{0:T(256)S(1)}, u32[256]{0:T(256)}, u32[]{:S(2)}) copy-start(u32[256]{0:T(256)} %constant.76) | copy-start | bytes 3076
  218.9 43.8 %collective-permute-start = (f32[80,272]{1,0:T(8,128)S(1)}, f32[80,272]{1,0:T(8,128)S(1)}, u32[]{:S(2)}, u32[]{:S(2)}) collective-permute-start(f32[80,272]{1,0:T(8,128)S(1)} %fusion), channel_id=1, source_target_pairs={{0,1},{1,2},{2,3},{3,4},{4,5},{5,6},{6,7},{7,8},{8,9},{9,10},{10,1... | collective-permute-start | bytes 261128
  222.6 40.2 %collective-permute-start.1 = (f32[80,272]{1,0:T(8,128)S(1)}, f32[80,272]{1,0:T(8,128)S(1)}, u32[]{:S(2)}, u32[]{:S(2)}) collective-permute-start(f32[80,272]{1,0:T(8,128)S(1)} %fusion), channel_id=1, source_target_pairs={{0,2},{1,3},{2,4},{3,5},{4,6},{5,7},{6,8},{7,9},{8,10},{9,11},{10,... | collective-permute-start | bytes 261128
  224.5 38.2 %collective-permute-start.2 = (f32[80,272]{1,0:T(8,128)S(1)}, f32[80,272]{1,0:T(8,128)S(1)}, u32[]{:S(2)}, u32[]{:S(2)}) collective-permute-start(f32[80,272]{1,0:T(8,128)S(1)} %fusion), channel_id=1, source_target_pairs={{0,3},{1,4},{2,5},{3,6},{4,7},{5,8},{6,9},{7,10},{8,11},{9,12},{10... | collective-permute-start | bytes 261128
  234.0 28.7 %collective-permute-start.3 = (f32[80,272]{1,0:T(8,128)S(1)}, f32[80,272]{1,0:T(8,128)S(1)}, u32[]{:S(2)}, u32[]{:S(2)}) collective-permute-start(f32[80,272]{1,0:T(8,128)S(1)} %fusion), channel_id=1, source_target_pairs={{0,4},{1,5},{2,6},{3,7},{4,8},{5,9},{6,10},{7,11},{8,12},{9,13},{1... | collective-permute-start | bytes 261128
  236.0 26.8 %collective-permute-start.4 = (f32[52,272]{1,0:T(8,128)S(1)}, f32[52,272]{1,0:T(8,128)S(1)}, u32[]{:S(2)}, u32[]{:S(2)}) collective-permute-start(f32[52,272]{1,0:T(8,128)S(1)} %slice.42), channel_id=1, source_target_pairs={{0,5},{1,6},{2,7},{3,8},{4,9},{5,10},{6,11},{7,12},{8,13},{9,14},{... | collective-permute-start | bytes 169736
Sparse Core Ops, SparseCore 0:
  68.7 66.2 all-gather.1
